TPU v7x, 32 devices: a whole 2x2x4 slice. The times are simulated.
32 devices in a mesh: fsdp: 4 (over z), ctx: 2 (over y), tp: 4 (over x, core).
Axes of the slice: x: 2, y: 2, z: 4, core: 2. Of those that a mesh axis runs over, the one named last changes fastest.
Arguments:
- block_input: bfloat16 [8, 2048, 1024], P('fsdp', 'ctx', 'tp'), may hold values from -45 to 45
- positions: int32 [8, 2048], P('fsdp', 'ctx'), may hold values from 0 to 2047, as said below
- first_gain: bfloat16 [1024], P('fsdp'), may hold values from 0.5 to 1.5
- first_shift: bfloat16 [1024], P('fsdp'), may hold values from -3 to 3
- second_gain: bfloat16 [1024], P('fsdp'), may hold values from 0.5 to 1.5
- second_shift: bfloat16 [1024], P('fsdp'), may hold values from -3 to 3
- triple_weight: bfloat16 [1024, 3, 1024], P('fsdp', None, 'tp'), as said below
- triple_bias: bfloat16 [3, 16, 64], P(None, 'tp', 'fsdp'), may hold values from -64 to 64
- mixer_weight: bfloat16 [1024, 1024], P('tp', 'fsdp'), may hold values from -2 to 2
- output_bias: bfloat16 [1024], P('fsdp'), may hold values from -3 to 3
- widen_weight: bfloat16 [1024, 4096], P('fsdp', 'tp'), may hold values from -0.1875 to 0.1875
- widen_bias: bfloat16 [32, 128], P('tp', 'fsdp'), may hold values from -3 to 3
- narrow_weight: bfloat16 [4096, 1024], P('tp', 'fsdp'), may hold values from -0.09375 to 0.09375
- cotangent: bfloat16 [8, 2048, 1024], P('fsdp', 'ctx', 'tp'), may hold values from -6 to 6
Outputs:
- block_output: bfloat16 [8, 2048, 1024], P('fsdp', 'ctx', 'tp')
- input_grad: bfloat16 [8, 2048, 1024], P('fsdp', 'ctx', 'tp')
- first_gain_grad: float32 [1024], P('fsdp')
- first_shift_grad: float32 [1024], P('fsdp')
- second_gain_grad: float32 [1024], P('fsdp')
- second_shift_grad: float32 [1024], P('fsdp')
- triple_weight_grad: float32 [1024, 3, 1024], P('fsdp', None, 'tp')
- triple_bias_grad: float32 [3, 16, 64], P(None, 'tp', 'fsdp')
- mixer_weight_grad: float32 [1024, 1024], P('tp', 'fsdp')
- output_bias_grad: float32 [1024], P('fsdp')
- widen_weight_grad: float32 [1024, 4096], P('fsdp', 'tp')
- widen_bias_grad: float32 [32, 128], P('tp', 'fsdp')
- narrow_weight_grad: float32 [4096, 1024], P('tp', 'fsdp')
Inputs may be any that keep to these rules, and one draw needn't show every extreme that they name: `positions`: each row counts up by one from 0 and falls back to 0 where a packed document begins; a row holds at most four documents; the first sequence is one whole document. `triple_weight`: entries are at most 4 / sqrt(1024) in magnitude.
All inputs are finite; a program needn't handle non-finite values.
Results may differ from a plain program's by a relative error of at most 0.017.
Values may be sent and summed in bfloat16 or wider, within the bound.
A program may use at most 192 MiB of HBM per device.

v0:
```python
import math

import jax
import jax.numpy as jnp
from jax import lax
from jax.sharding import PartitionSpec as P

ROT = 16


norm_eps = 1e-05
masked_score = -1e30


def normalize(rows):
    centred = rows - jnp.mean(rows, axis=-1, keepdims=True)
    inverse = lax.rsqrt(jnp.mean(centred * centred, axis=-1, keepdims=True) + norm_eps)
    return (centred * inverse, inverse)


def gelu_parts(widened):
    cumulative = 0.5 * (1.0 + lax.erf(widened * (1.0 / math.sqrt(2.0))))
    density = jnp.exp(-0.5 * widened * widened) * (1.0 / math.sqrt(2.0 * math.pi))
    return (widened * cumulative, cumulative + widened * density)


def rotary_tables(positions, rotary):
    half = rotary // 2
    freqs = jnp.exp(jnp.arange(half, dtype=jnp.float32) * (-2.0 * math.log(10000.0) / rotary))
    angles = positions.astype(jnp.float32)[:, None, :] * freqs[None, :, None]
    return (jnp.cos(angles)[:, None, None], jnp.sin(angles)[:, None, None])


def rotate_forward(block, cosine, sine, half):
    first = block[..., :half, :]
    second = block[..., half : 2 * half, :]
    return jnp.concatenate(
        [first * cosine - second * sine, second * cosine + first * sine, block[..., 2 * half :, :]],
        axis=-2,
    )


def rotate_back(block, cosine, sine, half):
    first = block[..., :half, :]
    second = block[..., half : 2 * half, :]
    return jnp.concatenate(
        [first * cosine + second * sine, second * cosine - first * sine, block[..., 2 * half :, :]],
        axis=-2,
    )


def masked_scores(queries, keys_in, item_positions, start, block, scale):
    length = keys_in.shape[2]
    index = jnp.arange(length, dtype=jnp.int32)
    rows = start + jnp.arange(block, dtype=jnp.int32)
    row_positions = lax.dynamic_slice_in_dim(item_positions, start, block, 1)
    gap_index = rows[:, None] - index[None, :]
    gap_positions = row_positions[:, :, None] - item_positions[:, None, :]
    visible = (gap_index >= 0)[None] & (gap_positions == gap_index[None])
    query_block = lax.dynamic_slice_in_dim(queries, start, block, 2)
    scores = (
        jnp.einsum("idq,idk->iqk", query_block, keys_in, preferred_element_type=jnp.float32) * scale
    )
    return (jnp.where(visible, scores, masked_score), query_block)


def attend_forward(queries, keys_in, values_in, item_positions, scale):
    items, head_size, length = queries.shape
    block = min(512, length)

    def step(number, carry):
        mixed_all, logsum_all = carry
        start = number * block
        scores, unused = masked_scores(queries, keys_in, item_positions, start, block, scale)
        top = jnp.max(scores, axis=2, keepdims=True)
        logsum = top + jnp.log(jnp.sum(jnp.exp(scores - top), axis=2, keepdims=True))
        weights = jnp.exp(scores - logsum).astype(jnp.bfloat16)
        mixed = jnp.einsum(
            "iqk,idk->idq", weights, values_in, preferred_element_type=jnp.float32
        ).astype(jnp.bfloat16)
        mixed_all = lax.dynamic_update_slice_in_dim(mixed_all, mixed, start, 2)
        logsum_all = lax.dynamic_update_slice_in_dim(logsum_all, logsum[:, :, 0], start, 1)
        return (mixed_all, logsum_all)

    start_state = (
        jnp.zeros((items, head_size, length), jnp.bfloat16),
        jnp.zeros((items, length), jnp.float32),
    )
    return lax.fori_loop(0, length // block, step, start_state)


def attend_backward(queries, keys_in, values_in, mixed, logsum, mixed_grad, item_positions, scale):
    items, head_size, length = queries.shape
    block = min(512, length)
    delta = jnp.sum(mixed_grad.astype(jnp.float32) * mixed.astype(jnp.float32), axis=1)

    def step(number, carry):
        query_grads, key_grads, value_grads = carry
        start = number * block
        scores, query_block = masked_scores(queries, keys_in, item_positions, start, block, scale)
        probs = jnp.exp(scores - lax.dynamic_slice_in_dim(logsum, start, block, 1)[:, :, None])
        grad_block = lax.dynamic_slice_in_dim(mixed_grad, start, block, 2)
        value_grads = value_grads + jnp.einsum(
            "iqk,idq->idk",
            probs.astype(jnp.bfloat16),
            grad_block,
            preferred_element_type=jnp.float32,
        )
        prob_grads = jnp.einsum(
            "idq,idk->iqk", grad_block, values_in, preferred_element_type=jnp.float32
        )
        delta_block = lax.dynamic_slice_in_dim(delta, start, block, 1)
        score_grads = (probs * (prob_grads - delta_block[:, :, None])).astype(jnp.bfloat16)
        query_part = (
            jnp.einsum("iqk,idk->idq", score_grads, keys_in, preferred_element_type=jnp.float32)
            * scale
        ).astype(jnp.bfloat16)
        query_grads = lax.dynamic_update_slice_in_dim(query_grads, query_part, start, 2)
        key_grads = key_grads + jnp.einsum(
            "iqk,idq->idk", score_grads, query_block, preferred_element_type=jnp.float32
        )
        return (query_grads, key_grads, value_grads)

    start_state = (
        jnp.zeros((items, head_size, length), jnp.bfloat16),
        jnp.zeros((items, head_size, length), jnp.float32),
        jnp.zeros((items, head_size, length), jnp.float32),
    )
    query_grads, key_grads, value_grads = lax.fori_loop(0, length // block, step, start_state)
    return (query_grads, (key_grads * scale).astype(jnp.bfloat16), value_grads.astype(jnp.bfloat16))


def norm_back_slice(grad, gain, normed, inverse, start, count):
    scaled = grad * gain
    mean_scaled = jnp.mean(scaled, axis=-1, keepdims=True)
    mean_cross = jnp.mean(scaled * normed, axis=-1, keepdims=True)
    scaled_part = lax.dynamic_slice_in_dim(scaled, start, count, 2)
    normed_part = lax.dynamic_slice_in_dim(normed, start, count, 2)
    return inverse * (scaled_part - mean_scaled - normed_part * mean_cross)


def shards(
    block_input,
    positions,
    first_gain,
    first_shift,
    second_gain,
    second_shift,
    triple_weight,
    triple_bias,
    mixer_weight,
    output_bias,
    widen_weight,
    widen_bias,
    narrow_weight,
    cotangent,
):
    gathered = (
        lax.all_gather(first_gain, "fsdp", axis=0, tiled=True),
        lax.all_gather(first_shift, "fsdp", axis=0, tiled=True),
        lax.all_gather(second_gain, "fsdp", axis=0, tiled=True),
        lax.all_gather(second_shift, "fsdp", axis=0, tiled=True),
        lax.all_gather(triple_weight, "fsdp", axis=0, tiled=True),
        lax.all_gather(triple_bias, "fsdp", axis=2, tiled=True),
        lax.all_gather(mixer_weight, "fsdp", axis=1, tiled=True),
        lax.all_gather(output_bias, "fsdp", axis=0, tiled=True),
        lax.all_gather(widen_weight, "fsdp", axis=0, tiled=True),
        lax.all_gather(widen_bias, "fsdp", axis=1, tiled=True),
        lax.all_gather(narrow_weight, "fsdp", axis=1, tiled=True),
    )
    (
        gain_first,
        shift_first,
        gain_second,
        shift_second,
        weight_triple,
        bias_triple,
        weight_mixer,
        bias_output,
        weight_widen,
        bias_widen,
        weight_narrow,
    ) = gathered
    seqs, local_tokens, local_width = block_input.shape
    width = weight_triple.shape[0]
    heads_local = bias_triple.shape[1]
    head_size = bias_triple.shape[2]
    hidden_local = weight_widen.shape[1]
    feature_start = lax.axis_index("tp") * local_width
    scale = head_size ** (-0.5)
    half = ROT // 2
    gain_one = gain_first.astype(jnp.float32)
    gain_two = gain_second.astype(jnp.float32)
    whole_input = lax.all_gather(block_input, "tp", axis=2, tiled=True)
    normed, inverse = normalize(whole_input.astype(jnp.float32))
    first_rows = (normed * gain_one + shift_first.astype(jnp.float32)).astype(jnp.bfloat16)
    second_rows = (normed * gain_two + shift_second.astype(jnp.float32)).astype(jnp.bfloat16)
    cosine, sine = rotary_tables(positions, ROT)
    weight_four = weight_triple.reshape(width, 3, heads_local, head_size)
    projected = jnp.einsum(
        "std,dchk->shckt", first_rows, weight_four, preferred_element_type=jnp.float32
    )
    projected = (
        projected + jnp.transpose(bias_triple.astype(jnp.float32), (1, 0, 2))[None, :, :, :, None]
    )
    turned = rotate_forward(projected[:, :, :2], cosine, sine, half)
    triple = jnp.concatenate([turned, projected[:, :, 2:]], axis=2).astype(jnp.bfloat16)
    packed = triple.reshape(seqs * heads_local, 3, head_size, local_tokens)
    by_heads = lax.all_to_all(packed, "ctx", split_axis=0, concat_axis=3, tiled=True)
    items = by_heads.shape[0]
    all_positions = lax.all_gather(positions, "ctx", axis=1, tiled=True)
    item_seq = (lax.axis_index("ctx") * items + jnp.arange(items, dtype=jnp.int32)) // heads_local
    item_positions = jnp.take(all_positions, item_seq, axis=0)
    queries = by_heads[:, 0]
    keys_in = by_heads[:, 1]
    values_in = by_heads[:, 2]
    mixed, logsum = attend_forward(queries, keys_in, values_in, item_positions, scale)
    mixed_tokens = lax.all_to_all(mixed, "ctx", split_axis=2, concat_axis=0, tiled=True).reshape(
        seqs, heads_local, head_size, local_tokens
    )
    mixer_four = weight_mixer.reshape(heads_local, head_size, width)
    attention_part = jnp.einsum(
        "shkt,hke->ste", mixed_tokens, mixer_four, preferred_element_type=jnp.float32
    )
    widened = jnp.einsum(
        "std,df->stf", second_rows, weight_widen, preferred_element_type=jnp.float32
    ) + bias_widen.reshape(hidden_local).astype(jnp.float32)
    activated_float, slope = gelu_parts(widened)
    activated = activated_float.astype(jnp.bfloat16)
    branches = attention_part + jnp.einsum(
        "stf,fe->ste", activated, weight_narrow, preferred_element_type=jnp.float32
    )
    summed = lax.psum_scatter(
        branches.astype(jnp.bfloat16), "tp", scatter_dimension=2, tiled=True
    ).astype(jnp.float32)
    bias_slice = lax.dynamic_slice_in_dim(bias_output, feature_start, local_width, 0).astype(
        jnp.float32
    )
    block_output = (block_input.astype(jnp.float32) + summed + bias_slice).astype(jnp.bfloat16)
    whole_cot = lax.all_gather(cotangent, "tp", axis=2, tiled=True)
    output_bias_grad = jnp.sum(whole_cot.astype(jnp.float32), axis=(0, 1))
    narrow_grad = jnp.einsum(
        "stf,ste->fe", activated, whole_cot, preferred_element_type=jnp.float32
    )
    hidden_grad = (
        jnp.einsum("ste,fe->stf", whole_cot, weight_narrow, preferred_element_type=jnp.float32)
        * slope
    )
    widen_bias_grad = jnp.sum(hidden_grad, axis=(0, 1)).reshape(bias_widen.shape)
    hidden_rounded = hidden_grad.astype(jnp.bfloat16)
    widen_grad = jnp.einsum(
        "std,stf->df", second_rows, hidden_rounded, preferred_element_type=jnp.float32
    )
    second_grad = jnp.einsum(
        "stf,df->std", hidden_rounded, weight_widen, preferred_element_type=jnp.float32
    )
    mixer_grad = jnp.einsum(
        "shkt,ste->hke", mixed_tokens, whole_cot, preferred_element_type=jnp.float32
    ).reshape(weight_mixer.shape)
    mixed_grad = jnp.einsum(
        "ste,hke->shkt", whole_cot, mixer_four, preferred_element_type=jnp.float32
    ).astype(jnp.bfloat16)
    mixed_grad = mixed_grad.reshape(seqs * heads_local, head_size, local_tokens)
    grad_heads = lax.all_to_all(mixed_grad, "ctx", split_axis=0, concat_axis=2, tiled=True)
    query_grads, key_grads, value_grads = attend_backward(
        queries, keys_in, values_in, mixed, logsum, grad_heads, item_positions, scale
    )
    stacked = jnp.stack([query_grads, key_grads, value_grads], axis=1)
    back_tokens = lax.all_to_all(stacked, "ctx", split_axis=3, concat_axis=0, tiled=True).reshape(
        seqs, heads_local, 3, head_size, local_tokens
    )
    back_float = back_tokens.astype(jnp.float32)
    unturned = rotate_back(back_float[:, :, :2], cosine, sine, half)
    projected_grad = jnp.concatenate([unturned, back_float[:, :, 2:]], axis=2)
    triple_bias_grad = jnp.transpose(jnp.sum(projected_grad, axis=(0, 4)), (1, 0, 2))
    projected_rounded = projected_grad.astype(jnp.bfloat16)
    triple_grad = jnp.einsum(
        "std,shckt->dchk", first_rows, projected_rounded, preferred_element_type=jnp.float32
    ).reshape(weight_triple.shape)
    first_grad = jnp.einsum(
        "shckt,dchk->std", projected_rounded, weight_four, preferred_element_type=jnp.float32
    )
    first_grad, second_grad = (
        lax.psum(first_grad.astype(jnp.bfloat16), "tp").astype(jnp.float32),
        lax.psum(second_grad.astype(jnp.bfloat16), "tp").astype(jnp.float32),
    )
    first_gain_grad = jnp.sum(first_grad * normed, axis=(0, 1))
    first_shift_grad = jnp.sum(first_grad, axis=(0, 1))
    second_gain_grad = jnp.sum(second_grad * normed, axis=(0, 1))
    second_shift_grad = jnp.sum(second_grad, axis=(0, 1))
    rows_grad = (
        cotangent.astype(jnp.float32)
        + norm_back_slice(first_grad, gain_one, normed, inverse, feature_start, local_width)
        + norm_back_slice(second_grad, gain_two, normed, inverse, feature_start, local_width)
    )
    input_grad = rows_grad.astype(jnp.bfloat16)
    shares = (
        lax.psum_scatter(
            first_gain_grad.astype(jnp.bfloat16), "fsdp", scatter_dimension=0, tiled=True
        ).astype(jnp.float32),
        lax.psum_scatter(
            first_shift_grad.astype(jnp.bfloat16), "fsdp", scatter_dimension=0, tiled=True
        ).astype(jnp.float32),
        lax.psum_scatter(
            second_gain_grad.astype(jnp.bfloat16), "fsdp", scatter_dimension=0, tiled=True
        ).astype(jnp.float32),
        lax.psum_scatter(
            second_shift_grad.astype(jnp.bfloat16), "fsdp", scatter_dimension=0, tiled=True
        ).astype(jnp.float32),
        lax.psum_scatter(
            triple_grad.astype(jnp.bfloat16), "fsdp", scatter_dimension=0, tiled=True
        ).astype(jnp.float32),
        lax.psum_scatter(
            triple_bias_grad.astype(jnp.bfloat16), "fsdp", scatter_dimension=2, tiled=True
        ).astype(jnp.float32),
        lax.psum_scatter(
            mixer_grad.astype(jnp.bfloat16), "fsdp", scatter_dimension=1, tiled=True
        ).astype(jnp.float32),
        lax.psum_scatter(
            output_bias_grad.astype(jnp.bfloat16), "fsdp", scatter_dimension=0, tiled=True
        ).astype(jnp.float32),
        lax.psum_scatter(
            widen_grad.astype(jnp.bfloat16), "fsdp", scatter_dimension=0, tiled=True
        ).astype(jnp.float32),
        lax.psum_scatter(
            widen_bias_grad.astype(jnp.bfloat16), "fsdp", scatter_dimension=1, tiled=True
        ).astype(jnp.float32),
        lax.psum_scatter(
            narrow_grad.astype(jnp.bfloat16), "fsdp", scatter_dimension=1, tiled=True
        ).astype(jnp.float32),
    )
    (
        share_a,
        share_b,
        share_c,
        share_d,
        share_e,
        share_f,
        share_g,
        share_h,
        share_i,
        share_j,
        share_k,
    ) = shares
    reduced = (
        lax.psum(share_a.astype(jnp.bfloat16), "ctx").astype(jnp.float32),
        lax.psum(share_b.astype(jnp.bfloat16), "ctx").astype(jnp.float32),
        lax.psum(share_c.astype(jnp.bfloat16), "ctx").astype(jnp.float32),
        lax.psum(share_d.astype(jnp.bfloat16), "ctx").astype(jnp.float32),
        lax.psum(share_e.astype(jnp.bfloat16), "ctx").astype(jnp.float32),
        lax.psum(share_f.astype(jnp.bfloat16), "ctx").astype(jnp.float32),
        lax.psum(share_g.astype(jnp.bfloat16), "ctx").astype(jnp.float32),
        lax.psum(share_h.astype(jnp.bfloat16), "ctx").astype(jnp.float32),
        lax.psum(share_i.astype(jnp.bfloat16), "ctx").astype(jnp.float32),
        lax.psum(share_j.astype(jnp.bfloat16), "ctx").astype(jnp.float32),
        lax.psum(share_k.astype(jnp.bfloat16), "ctx").astype(jnp.float32),
    )
    return (
        block_output,
        input_grad,
        reduced[0],
        reduced[1],
        reduced[2],
        reduced[3],
        reduced[4],
        reduced[5],
        reduced[6],
        reduced[7],
        reduced[8],
        reduced[9],
        reduced[10],
    )


def solution(mesh):
    in_specs = (
        P("fsdp", "ctx", "tp"),
        P("fsdp", "ctx"),
        P("fsdp"),
        P("fsdp"),
        P("fsdp"),
        P("fsdp"),
        P("fsdp", None, "tp"),
        P(None, "tp", "fsdp"),
        P("tp", "fsdp"),
        P("fsdp"),
        P("fsdp", "tp"),
        P("tp", "fsdp"),
        P("tp", "fsdp"),
        P("fsdp", "ctx", "tp"),
    )
    out_specs = (
        P("fsdp", "ctx", "tp"),
        P("fsdp", "ctx", "tp"),
        P("fsdp"),
        P("fsdp"),
        P("fsdp"),
        P("fsdp"),
        P("fsdp", None, "tp"),
        P(None, "tp", "fsdp"),
        P("tp", "fsdp"),
        P("fsdp"),
        P("fsdp", "tp"),
        P("tp", "fsdp"),
        P("tp", "fsdp"),
    )
    return jax.shard_map(shards, mesh=mesh, in_specs=in_specs, out_specs=out_specs, check_vma=False)
```

profile of v0, /device:TPU:0, one launch (start us, length us, event | category | flops | bytes accessed | tf_op | source)
XLA Modules:
  0.0 982.9 jit_solution(4454714887823172964)
XLA Ops:
  17.6 12.0 %all-gather = bf16[4,1,256]{2,1,0:T(2,128)(2,1)S(1)} all-gather(bf16[1,1,256]{2,1,0:T(2,128)(2,1)S(1)} %reshape.291), channel_id=1, replica_groups=mesh['fsdp'=4,'ctx'=2,'tp'=4] {'fsdp'}, dimensions={0}, use_global_device_ids=true | all-gather | bytes 2560 | tf_op jit(solution)/shard_map/all_gather | solution.py:159
  39.0 13.6 %all_gather.47 = bf16[3,4,64]{1,0,2:T(4,128)(2,1)S(1)} all-gather(bf16[3,4,16]{1,0,2:T(4,128)(2,1)S(1)} %copy.87), channel_id=1, replica_groups=mesh['fsdp'=4,'ctx'=2,'tp'=4] {'fsdp'}, dimensions={2}, use_global_device_ids=true | all-gather | bytes 1920 | tf_op jit(solution)/shard_map/all_gather | solution.py:164
  55.3 30.4 %all-gather.12.cloned.1.call-done = bf16[2,1024,1024]{2,1,0:T(8,128)(2,1)} async-done(((bf16[2,1024,256]{2,1,0:T(8,128)(2,1)}), bf16[2,1024,1024]{2,1,0:T(8,128)(2,1)}) %all-gather.12.cloned.1.call-update) | async-done | bytes 4194320 | tf_op jit(solution)/shard_map/all_gather | solution.py:194
  112.8 12.6 %all-gather.4 = bf16[4,32,8]{1,2,0:T(8,128)(2,1)S(1)} all-gather(bf16[1,32,8]{1,2,0:T(8,128)(2,1)S(1)} %bitcast.235), channel_id=1, replica_groups=mesh['fsdp'=4,'ctx'=2,'tp'=4] {'fsdp'}, dimensions={0}, use_global_device_ids=true | all-gather | bytes 2560 | tf_op jit(solution)/shard_map/all_gather | solution.py:168
  146.4 111.9 %while.33 = (s32[]{:T(128)}, bf16[4,64,2048]{2,1,0:T(8,128)(2,1)}, f32[4,2048]{1,0:T(4,128)S(1)}, s32[4,2048]{1,0:T(4,128)S(1)}, bf16[4,64,2048]{2,1,0:T(8,128)(...) while((s32[]{:T(128)}, bf16[4,64,2048]{2,1,0:T(8,128)(2,1)}, ...), condition=%wide.region_5.6_spmd, body=%wide.region_2.0_spmd.sunk | while | flops 1118960128 | bytes 63568048 | solution.py:89
  262.6 15.6 %reshape.332 = bf16[2,2,131072]{2,1,0:T(2,128)(2,1)} reshape(bf16[2048,4,64]{2,1,0:T(4,128)(2,1)} %bitcast.204) | data formatting | bytes 2097152
  282.8 12.8 %fusion.83 = (bf16[1024]{0:T(1024)(128)(2,1)}, bf16[2,1024,1024]{2,1,0:T(8,128)(2,1)}) fusion(f32[2,1024,1024]{2,1,0:T(8,128)} %get-tuple-element.498, f32[1024]{0:T(1024)S(1)} %bitcast.229, bf16[2,1024,1024]{2,1,0:T(8,128)(2,1)} %all-gather.20.cloned.1.call-done, bf16[1024,1024]{1,0:T(8,128)(2,1)} %all-gather.18.cloned.1.call-done), kind=kOutput, calls=%fused_computation.153 | convolution fusion | flops 4320132096 | bytes 18880512 | tf_op jit(solution)/shard_map/ste,fe->stf/dot_general | solution.py:246
  315.9 17.8 %all_gather.48 = bf16[256,1024]{1,0:T(8,128)(2,1)S(1)} all-gather(bf16[256,256]{1,0:T(8,128)(2,1)S(1)} %copy-done.29), channel_id=1, replica_groups=mesh['fsdp'=4,'ctx'=2,'tp'=4] {'fsdp'}, dimensions={1}, use_global_device_ids=true | all-gather | bytes 655360 | tf_op jit(solution)/shard_map/all_gather | solution.py:165
  359.5 193.2 %while.34 = (s32[]{:T(128)}, bf16[4,64,2048]{2,1,0:T(8,128)(2,1)}, f32[4,64,2048]{2,1,0:T(8,128)S(1)}, f32[4,64,2048]{2,1,0:T(8,128)}, s32[4,2048]{1,0:T(4,128)S...) while((s32[]{:T(128)}, bf16[4,64,2048]{2,1,0:T(8,128)(2,1)}, ...), condition=%wide.region_9.10_spmd.clone, body=%wide.region_8.9_spmd.clone.sunk | while | flops 2756968960 | bytes 183925168 | solution.py:129
  372.0 14.2 %multiply_convert_fusion.4 = bf16[4,512,2048]{2,1,0:T(8,128)(2,1)} fusion(f32[4,512,2048]{2,1,0:T(8,128)} %fusion.133, f32[4,512]{1,0:T(4,128)S(1)} %get-tuple-element.627, f32[4,512]{1,0:T(4,128)S(1)} %get-tuple-element.628, s32[512,2048]{1,0:T(8,128)S(1)} %iota_subtract_fusion.5, s32[4,2048]{1,0:T(4,128)S(1)} %get-tuple-element.696, ...), kind=kOutput, calls=%fused_computation.19.clone.1 | convolution fusion | flops 574619648 | bytes 31776772 | tf_op jit(solution)/shard_map/while/body/eval_jaxpr/idq,idk->iqk/dot_general | solution.py:109
  395.7 12.0 %fusion.135 = f32[4,64,2048]{2,1,0:T(8,128)} fusion(f32[4,512,2048]{2,1,0:T(8,128)} %fusion.133, f32[4,512]{1,0:T(4,128)S(1)} %get-tuple-element.628, s32[512,2048]{1,0:T(8,128)S(1)} %copy-done.2, s32[4,2048]{1,0:T(4,128)S(1)} %get-tuple-element.696, s32[4,512]{1,0:T(4,128)S(1)} %constant_dynamic-slice_fusion.9, ...), kind=kOutput, calls=%fused_computation.28.clone.1 | convolution fusion | flops 567279616 | bytes 26525700 | tf_op jit(solution)/shard_map/while/body/eval_jaxpr/iqk,idq->idk/dot_general | solution.py:103
  419.9 14.1 %multiply_convert_fusion.4 = bf16[4,512,2048]{2,1,0:T(8,128)(2,1)} fusion(f32[4,512,2048]{2,1,0:T(8,128)} %fusion.133, f32[4,512]{1,0:T(4,128)S(1)} %get-tuple-element.627, f32[4,512]{1,0:T(4,128)S(1)} %get-tuple-element.628, s32[512,2048]{1,0:T(8,128)S(1)} %iota_subtract_fusion.5, s32[4,2048]{1,0:T(4,128)S(1)} %get-tuple-element.696, ...), kind=kOutput, calls=%fused_computation.19.clone.1 | convolution fusion | flops 574619648 | bytes 31776772 | tf_op jit(solution)/shard_map/while/body/eval_jaxpr/idq,idk->iqk/dot_general | solution.py:109
  443.4 12.6 %fusion.135 = f32[4,64,2048]{2,1,0:T(8,128)} fusion(f32[4,512,2048]{2,1,0:T(8,128)} %fusion.133, f32[4,512]{1,0:T(4,128)S(1)} %get-tuple-element.628, s32[512,2048]{1,0:T(8,128)S(1)} %copy-done.2, s32[4,2048]{1,0:T(4,128)S(1)} %get-tuple-element.696, s32[4,512]{1,0:T(4,128)S(1)} %constant_dynamic-slice_fusion.9, ...), kind=kOutput, calls=%fused_computation.28.clone.1 | convolution fusion | flops 567279616 | bytes 26525700 | tf_op jit(solution)/shard_map/while/body/eval_jaxpr/iqk,idq->idk/dot_general | solution.py:103
  468.1 14.1 %multiply_convert_fusion.4 = bf16[4,512,2048]{2,1,0:T(8,128)(2,1)} fusion(f32[4,512,2048]{2,1,0:T(8,128)} %fusion.133, f32[4,512]{1,0:T(4,128)S(1)} %get-tuple-element.627, f32[4,512]{1,0:T(4,128)S(1)} %get-tuple-element.628, s32[512,2048]{1,0:T(8,128)S(1)} %iota_subtract_fusion.5, s32[4,2048]{1,0:T(4,128)S(1)} %get-tuple-element.696, ...), kind=kOutput, calls=%fused_computation.19.clone.1 | convolution fusion | flops 574619648 | bytes 31776772 | tf_op jit(solution)/shard_map/while/body/eval_jaxpr/idq,idk->iqk/dot_general | solution.py:109
  491.7 12.6 %fusion.135 = f32[4,64,2048]{2,1,0:T(8,128)} fusion(f32[4,512,2048]{2,1,0:T(8,128)} %fusion.133, f32[4,512]{1,0:T(4,128)S(1)} %get-tuple-element.628, s32[512,2048]{1,0:T(8,128)S(1)} %copy-done.2, s32[4,2048]{1,0:T(4,128)S(1)} %get-tuple-element.696, s32[4,512]{1,0:T(4,128)S(1)} %constant_dynamic-slice_fusion.9, ...), kind=kOutput, calls=%fused_computation.28.clone.1 | convolution fusion | flops 567279616 | bytes 26525700 | tf_op jit(solution)/shard_map/while/body/eval_jaxpr/iqk,idq->idk/dot_general | solution.py:103
  516.4 14.1 %multiply_convert_fusion.4 = bf16[4,512,2048]{2,1,0:T(8,128)(2,1)} fusion(f32[4,512,2048]{2,1,0:T(8,128)} %fusion.133, f32[4,512]{1,0:T(4,128)S(1)} %get-tuple-element.627, f32[4,512]{1,0:T(4,128)S(1)} %get-tuple-element.628, s32[512,2048]{1,0:T(8,128)S(1)} %iota_subtract_fusion.5, s32[4,2048]{1,0:T(4,128)S(1)} %get-tuple-element.696, ...), kind=kOutput, calls=%fused_computation.19.clone.1 | convolution fusion | flops 574619648 | bytes 31776772 | tf_op jit(solution)/shard_map/while/body/eval_jaxpr/idq,idk->iqk/dot_general | solution.py:109
  540.0 12.6 %fusion.135 = f32[4,64,2048]{2,1,0:T(8,128)} fusion(f32[4,512,2048]{2,1,0:T(8,128)} %fusion.133, f32[4,512]{1,0:T(4,128)S(1)} %get-tuple-element.628, s32[512,2048]{1,0:T(8,128)S(1)} %copy-done.2, s32[4,2048]{1,0:T(4,128)S(1)} %get-tuple-element.696, s32[4,512]{1,0:T(4,128)S(1)} %constant_dynamic-slice_fusion.9, ...), kind=kOutput, calls=%fused_computation.28.clone.1 | convolution fusion | flops 567279616 | bytes 26525700 | tf_op jit(solution)/shard_map/while/body/eval_jaxpr/iqk,idq->idk/dot_general | solution.py:103
  569.1 37.5 %all_to_all.60 = bf16[2,2,393216]{2,1,0:T(2,128)(2,1)} all-to-all(bf16[2,2,393216]{2,1,0:T(2,128)(2,1)S(1)} %reshape.330), channel_id=1, replica_groups=mesh['fsdp'=4,'ctx'=2,'tp'=4] {'ctx'}, dimensions={0} | all-to-all | bytes 6291456 | tf_op jit(solution)/shard_map/all_to_all | solution.py:269
  664.7 12.9 %reduce-scatter.14.cloned.1.call-done = bf16[256,3,256]{0,2,1:T(8,128)(2,1)} async-done(((bf16[1024,3,256]{0,2,1:T(8,128)(2,1)}), bf16[256,3,256]{0,2,1:T(8,128)(2,1)}) %reduce-scatter.14.cloned.1.call-update) | async-done | bytes 393232 | tf_op jit(solution)/shard_map/reduce_scatter | solution.py:310
  703.0 15.6 %reduce-scatter.22.cloned.1.call-done = bf16[16,12]{1,0:T(8,128)(2,1)} async-done(((bf16[64,12]{1,0:T(8,128)(2,1)}), bf16[16,12]{1,0:T(8,128)(2,1)}) %reduce-scatter.22.cloned.1.call-update) | async-done | bytes 400
  719.5 152.7 %all-reduce.12.cloned.1.call-done = (bf16[2,1024,1024]{2,1,0:T(8,128)(2,1)}, bf16[2,1024,1024]{2,1,0:T(8,128)(2,1)}) async-done(((bf16[2,1024,1024]{2,1,0:T(8,128)(2,1)}, bf16[2,1024,1024]{2,1,0:T(8,128)(2,1)}), (bf16[2,1024,1024]{2,1,0:T(8,128)(2,1)}, bf16[2,1024,1024]{2,1,0:T(8,128)(2,1)})) %all-reduce.12.cloned.1.call-update) | async-done | bytes 8388624 | tf_op jit(solution)/shard_map/psum | solution.py:285
  878.0 17.1 %fusion.34 = (bf16[1024]{0:T(1024)(128)(2,1)S(1)}, f32[2,1024]{1,0:T(2,128)S(1)}, f32[2,1024]{1,0:T(2,128)S(1)}, bf16[1024]{0:T(1024)(128)(2,1)S(1)}, f32[2,1024...) fusion(bf16[2,1024,1024]{2,1,0:T(8,128)(2,1)} %get-tuple-elemen, ...), kind=kLoop, calls=%fused_computation.60 | loop fusion | flops 35641344 | bytes 37810176 | tf_op jit(solution)/shard_map/reduce_sum | solution.py:289
  895.1 18.4 %all-reduce.6 = (bf16[1024]{0:T(1024)(128)(2,1)S(1)}, bf16[1024]{0:T(1024)(128)(2,1)S(1)}, bf16[1024]{0:T(1024)(128)(2,1)S(1)}, bf16[1024]{0:T(1024)(128)(2,1)S(1)}, bf16[1024]{0:T(1024)(128)(2,1)S(1)}) all-reduce(bf16[1024]{0:T(1024)(128)(2,1)S(1)} %get-tuple-element.422, ...), channel_id=3, replica_groups=mesh['fsdp'=4,'ctx'=2,'tp'=4] {'fsdp'}, use_global_device_ids=true, to_apply=%region_17.18.clone | all-reduce | flops 5120 | bytes 20480
  935.6 37.8 %reduce-scatter.12.cloned.1.call-done = bf16[2,1024,256]{2,1,0:T(8,128)(2,1)} async-done(((bf16[2,1024,1024]{2,1,0:T(8,128)(2,1)}), bf16[2,1024,256]{2,1,0:T(8,128)(2,1)}) %reduce-scatter.12.cloned.1.call-update) | async-done | bytes 1048592 | tf_op jit(solution)/shard_map/reduce_scatter | solution.py:233
  (349 shorter events, 453.1 us)
Async XLA Ops:
  7.2 46.4 %all-gather.14.cloned.1.call-start = ((), (), s32[]{:S(2)}) async-start(), calls=%async_computation.12 | async-start | bytes 1966080 | tf_op jit(solution)/shard_map/all_gather | solution.py:163
  7.9 77.8 %all-gather.12.cloned.1.call-start = ((), (), s32[]{:S(2)}) async-start(), calls=%async_computation.11 | async-start | bytes 5242880 | tf_op jit(solution)/shard_map/all_gather | solution.py:194
  8.7 125.0 %all-gather.16.cloned.1.call-start = ((), (), s32[]{:S(2)}) async-start(), calls=%async_computation.13 | async-start | bytes 2621440 | tf_op jit(solution)/shard_map/all_gather | solution.py:167
  9.4 273.4 %all-gather.18.cloned.1.call-start = ((), (), s32[]{:S(2)}) async-start(), calls=%async_computation.14 | async-start | bytes 2621440 | tf_op jit(solution)/shard_map/all_gather | solution.py:169
  10.0 272.8 %all-gather.20.cloned.1.call-start = ((), (), s32[]{:S(2)}) async-start(), calls=%async_computation.16 | async-start | bytes 5242880 | tf_op jit(solution)/shard_map/all_gather | solution.py:240
  29.6 61.0 %copy-start.35 = (f32[4,1,256]{2,1,0:T(1,128)}, f32[4,1,256]{2,1,0:T(1,128)S(1)}, u32[]{:S(2)}) copy-start(f32[4,1,256]{2,1,0:T(1,128)S(1)} %convert_element_type.305) | copy-start | bytes 12292
  38.2 52.5 %copy-start.39 = (f32[4,1,256]{2,1,0:T(1,128)}, f32[4,1,256]{2,1,0:T(1,128)S(1)}, u32[]{:S(2)}) copy-start(f32[4,1,256]{2,1,0:T(1,128)S(1)} %convert_element_type.306) | copy-start | bytes 12292
  89.2 216.6 %copy-start.33 = (f32[2,1024]{1,0:T(2,128)}, f32[2,1024]{1,0:T(2,128)S(1)}, u32[]{:S(2)}) copy-start(f32[2,1024]{1,0:T(2,128)S(1)} %broadcast_multiply_fusion.4) | copy-start | bytes 24580
  90.6 215.2 %copy-start.31 = (f32[2,1024]{1,0:T(2,128)}, f32[2,1024]{1,0:T(2,128)S(1)}, u32[]{:S(2)}) copy-start(f32[2,1024]{1,0:T(2,128)S(1)} %add_rsqrt_fusion) | copy-start | bytes 24580
  97.2 47.4 %all-to-all-start = ((bf16[8,3,64,1024]{3,2,1,0:T(8,128)(2,1)}), bf16[8,3,64,1024]{3,2,1,0:T(8,128)(2,1)S(1)}, u32[]{:S(2)}, u32[]{:S(2)}) async-start(bf16[8,3,64,1024]{3,2,1,0:T(8,128)(2,1)} %pad_maximum_fusion.1), calls=%async_computation | async-start | bytes 6291456 | tf_op jit(solution)/shard_map/all_to_all | solution.py:209
  112.8 193.0 %copy-start.37 = (f32[4,1,256]{2,1,0:T(1,128)}, f32[4,1,256]{2,1,0:T(1,128)S(1)}, u32[]{:S(2)}) copy-start(f32[4,1,256]{2,1,0:T(1,128)S(1)} %convert_element_type.307) | copy-start | bytes 12292
  278.3 17.9 %all-to-all-start.1 = ((bf16[2,2,131072]{2,1,0:T(2,128)(2,1)}), bf16[2,2,131072]{2,1,0:T(2,128)(2,1)}, u32[]{:S(2)}, u32[]{:S(2)}) async-start(bf16[2,2,131072]{2,1,0:T(2,128)(2,1)} %reshape.332), calls=%async_computation.1 | async-start | bytes 2097152 | tf_op jit(solution)/shard_map/all_to_all | solution.py:218
  282.7 382.0 %reduce-scatter.16.cloned.1.call-start = ((), (), s32[]{:S(2)}) async-start(), calls=%async_computation.18 | async-start | bytes 655360 | tf_op jit(solution)/shard_map/reduce_scatter | solution.py:316
  305.7 359.0 %reduce-scatter.18.cloned.1.call-start = ((), (), s32[]{:S(2)}) async-start(), calls=%async_computation.19 | async-start | bytes 2621440 | tf_op jit(solution)/shard_map/reduce_scatter | solution.py:322
  338.4 16.6 %all-to-all-start.2 = ((bf16[8,64,1024]{2,1,0:T(8,128)(2,1)}), bf16[8,64,1024]{2,1,0:T(8,128)(2,1)}, u32[]{:S(2)}, u32[]{:S(2)}) async-start(bf16[8,64,1024]{2,1,0:T(8,128)(2,1)} %bitcast.208), calls=%async_computation.3 | async-start | bytes 2097152 | tf_op jit(solution)/shard_map/all_to_all | solution.py:264
  342.9 321.9 %reduce-scatter.20.cloned.1.call-start = ((), (), s32[]{:S(2)}) async-start(), calls=%async_computation.20 | async-start | bytes 2621440 | tf_op jit(solution)/shard_map/reduce_scatter | solution.py:328
  352.4 325.3 %reduce-scatter.14.cloned.1.call-start = ((), (), s32[]{:S(2)}) async-start(), calls=%async_computation.17 | async-start | bytes 1966080 | tf_op jit(solution)/shard_map/reduce_scatter | solution.py:310
  644.4 57.8 %reduce-scatter.24.cloned.1.call-start = ((), (), s32[]{:S(2)}) async-start(), calls=%async_computation.22 | async-start | bytes 40960
  645.2 73.4 %reduce-scatter.22.cloned.1.call-start = ((), (), s32[]{:S(2)}) async-start(), calls=%async_computation.21 | async-start | bytes 20480
  656.7 215.5 %all-reduce.12.cloned.1.call-start = ((), (), s32[]{:S(2)}) async-start(), calls=%async_computation.23 | async-start | bytes 16777216 | tf_op jit(solution)/shard_map/psum | solution.py:285
  664.6 263.9 %all-reduce.14.cloned.1.call-start = ((), (), s32[]{:S(2)}) async-start(), calls=%async_computation.24 | async-start | bytes 3145728 | tf_op jit(solution)/shard_map/psum | solution.py:350
  677.7 295.7 %reduce-scatter.12.cloned.1.call-start = ((), (), s32[]{:S(2)}) async-start(), calls=%async_computation.15 | async-start | bytes 5242880 | tf_op jit(solution)/shard_map/reduce_scatter | solution.py:233
  878.0 45.3 %copy-start.16 = (bf16[2,1024,256]{2,1,0:T(8,128)(2,1)S(1)}, bf16[2,1024,256]{2,1,0:T(8,128)(2,1)}, u32[]{:S(2)}) copy-start(bf16[2,1024,256]{2,1,0:T(8,128)(2,1)} %param.31) | copy-start | bytes 3145732
  928.5 44.9 %copy-start.17 = (bf16[2,1024,256]{2,1,0:T(8,128)(2,1)S(1)}, bf16[2,1024,256]{2,1,0:T(8,128)(2,1)}, u32[]{:S(2)}) copy-start(bf16[2,1024,256]{2,1,0:T(8,128)(2,1)} %param.18) | copy-start | bytes 3145732
  (58 other events, 406.8 us)
Sparse Core Ops, SparseCore 0:
  9.6 40.7 all-gather.13
  51.9 33.8 all-gather.11
  87.3 45.9 all-gather.15
  134.7 45.0 all-gather.17
  181.2 33.1 all-gather.19
  305.8 22.1 reduce-scatter.15
  330.3 44.4 reduce-scatter.17
  377.1 42.8 reduce-scatter.19
  644.6 33.0 reduce-scatter.13
  680.3 18.0 reduce-scatter.23
  701.3 17.3 reduce-scatter.21
  721.1 151.0 all-reduce.11
  874.6 51.8 all-reduce.13
  929.0 44.3 reduce-scatter.11
where the time goes:
time: 990 us; the launch traced here: 983 us
  matrix products  340 us (34%)
  waiting for transfers between devices  256 us (26%)
  blocking collectives  159 us (16%)
  local copies, waits for them, and re-layouts  99 us (10%)
  other arithmetic  98.5 us (10%)
  between operations  15.8 us (2%)
  starting transfers between devices  13.7 us (1%)
    psum x1, waiting for transfers between devices, shards(): lax.psum(second_grad.astype(jnp.bfloat16), 'tp').astype(jnp.float32)  153 us
    dot_general x8, matrix products, masked_scores(): jnp.einsum('idq,idk->iqk', query_block, keys_in, preferred_element_type=j...  74.4 us
    dot_general x4, matrix products, step(): jnp.einsum('idq,idk->iqk', grad_block, values_in, preferred_element_type=...  56.5 us
    dot_general x4, matrix products, step(): jnp.einsum('iqk,idq->idk', probs.astype(jnp.bfloat16), grad_block, prefer...  49.8 us
    unnamed x106, local copies, waits for them, and re-layouts  45.9 us
    reduce_scatter x1, waiting for transfers between devices, shards(): lax.psum_scatter(branches.astype(jnp.bfloat16), 'tp', scatter_dimension=2...  37.8 us
    all_to_all x1, blocking collectives, shards(): lax.all_to_all(stacked, 'ctx', split_axis=3, concat_axis=0, tiled=True)  37.5 us
    dot_general x4, matrix products, step(): jnp.einsum('iqk,idk->idq', weights, values_in, preferred_element_type=jnp...  37 us
  transfers between devices with their start and end apart: 17, of which 7 were waited for; matrix products, arithmetic and copies ran while one was open for 52% of the time, Pallas kernels for 0%

commit v1 on v0

v1 whole, which is shorter than its diff:
```python
import functools
import math

import jax
import jax.numpy as jnp
from jax import lax
from jax.experimental import pallas as pl
from jax.experimental.pallas import tpu as pltpu
from jax.sharding import PartitionSpec as P

ROT = 16


norm_eps = 1e-05
masked_score = -1e30


def normalize(rows):
    centred = rows - jnp.mean(rows, axis=-1, keepdims=True)
    inverse = lax.rsqrt(jnp.mean(centred * centred, axis=-1, keepdims=True) + norm_eps)
    return (centred * inverse, inverse)


def gelu_parts(widened):
    cumulative = 0.5 * (1.0 + lax.erf(widened * (1.0 / math.sqrt(2.0))))
    density = jnp.exp(-0.5 * widened * widened) * (1.0 / math.sqrt(2.0 * math.pi))
    return (widened * cumulative, cumulative + widened * density)


def rotary_tables(positions, rotary):
    half = rotary // 2
    freqs = jnp.exp(jnp.arange(half, dtype=jnp.float32) * (-2.0 * math.log(10000.0) / rotary))
    angles = positions.astype(jnp.float32)[:, None, :] * freqs[None, :, None]
    return (jnp.cos(angles)[:, None, None], jnp.sin(angles)[:, None, None])


def rotate_forward(block, cosine, sine, half):
    first = block[..., :half, :]
    second = block[..., half : 2 * half, :]
    return jnp.concatenate(
        [first * cosine - second * sine, second * cosine + first * sine, block[..., 2 * half :, :]],
        axis=-2,
    )


def rotate_back(block, cosine, sine, half):
    first = block[..., :half, :]
    second = block[..., half : 2 * half, :]
    return jnp.concatenate(
        [first * cosine + second * sine, second * cosine - first * sine, block[..., 2 * half :, :]],
        axis=-2,
    )


def attend_kernel(block, scale, qkv_ref, grad_ref, base_ref, back_ref, mixed_ref,
                  queries, query_rows, keys, key_rows, values, value_rows, grads, grad_rows,
                  base_rows, key_sum, value_sum):
    parts, head_size, span = grad_ref.shape[0], grad_ref.shape[2], grad_ref.shape[3]
    length = parts * span
    for part in range(parts):
        at = pl.ds(part * span, span)
        queries[:, at] = (qkv_ref[part, 0, 0].astype(jnp.float32) * scale).astype(jnp.bfloat16)
        keys[:, at] = qkv_ref[part, 0, 1]
        values[:, at] = qkv_ref[part, 0, 2]
        grads[:, at] = grad_ref[part, 0]
    for source, target in (
        (queries, query_rows),
        (keys, key_rows),
        (values, value_rows),
        (grads, grad_rows),
    ):
        target[...] = source[...].astype(jnp.float32).T.astype(jnp.bfloat16)
    base_row = base_ref[0]
    base_rows[...] = jnp.broadcast_to(base_row, (128, length)).T
    for start in range(0, length, block):
        count = start + block
        here = slice(start, count)
        scores = jnp.dot(key_rows[:count], queries[:, here], preferred_element_type=jnp.float32)
        wide_base = jnp.concatenate([base_rows[:count]] * (block // 128), axis=1)
        same = wide_base == base_row[:, here]
        key_index = lax.broadcasted_iota(jnp.int32, (block, block), 0)
        query_index = lax.broadcasted_iota(jnp.int32, (block, block), 1)
        last = jnp.where(
            same[start:] & (key_index <= query_index), scores[start:], masked_score
        )
        if start:
            earlier = jnp.where(same[:start], scores[:start], masked_score)
            scores = jnp.concatenate([earlier, last], axis=0)
        else:
            scores = last
        top = jnp.max(scores, axis=0, keepdims=True)
        raised = jnp.exp(scores - top)
        probs = raised * (1.0 / jnp.sum(raised, axis=0, keepdims=True))
        weights = probs.astype(jnp.bfloat16)
        mixed = jnp.dot(values[:, :count], weights, preferred_element_type=jnp.float32).astype(
            jnp.bfloat16
        )
        grad_block = grads[:, here]
        delta = jnp.sum(
            mixed.astype(jnp.float32) * grad_block.astype(jnp.float32), axis=0, keepdims=True
        )
        prob_grads = jnp.dot(value_rows[:count], grad_block, preferred_element_type=jnp.float32)
        score_grads = (probs * (prob_grads - delta)).astype(jnp.bfloat16)
        query_part = jnp.dot(keys[:, :count], score_grads, preferred_element_type=jnp.float32)
        key_part = jnp.dot(score_grads, query_rows[here], preferred_element_type=jnp.float32)
        value_part = jnp.dot(weights, grad_rows[here], preferred_element_type=jnp.float32)
        if start:
            key_sum[:start] += key_part[:start]
            value_sum[:start] += value_part[:start]
        key_sum[here] = key_part[start:]
        value_sum[here] = value_part[start:]
        part, inside = start // span, start % span
        mixed_ref[part, 0, :, inside : inside + block] = mixed
        back_ref[part, 0, 0, :, inside : inside + block] = (query_part * scale).astype(jnp.bfloat16)
    for part in range(parts):
        at = pl.ds(part * span, span)
        back_ref[part, 0, 1] = key_sum[at].T.astype(jnp.bfloat16)
        back_ref[part, 0, 2] = value_sum[at].T.astype(jnp.bfloat16)


def attend(by_heads, grad_heads, item_base, scale):
    parts, items, unused, head_size, span = by_heads.shape
    length = parts * span
    block = min(256, span)
    wide = pltpu.VMEM((head_size, length), jnp.bfloat16)
    tall = pltpu.VMEM((length, head_size), jnp.bfloat16)
    total = pltpu.VMEM((length, head_size), jnp.float32)
    return pl.pallas_call(
        functools.partial(attend_kernel, block, scale),
        grid=(items,),
        in_specs=[
            pl.BlockSpec((parts, 1, 3, head_size, span), lambda i: (0, i, 0, 0, 0)),
            pl.BlockSpec((parts, 1, head_size, span), lambda i: (0, i, 0, 0)),
            pl.BlockSpec((1, 1, length), lambda i: (i, 0, 0)),
        ],
        out_specs=[
            pl.BlockSpec((parts, 1, 3, head_size, span), lambda i: (0, i, 0, 0, 0)),
            pl.BlockSpec((parts, 1, head_size, span), lambda i: (0, i, 0, 0)),
        ],
        out_shape=[
            jax.ShapeDtypeStruct(by_heads.shape, jnp.bfloat16),
            jax.ShapeDtypeStruct(grad_heads.shape, jnp.bfloat16),
        ],
        scratch_shapes=[wide, tall, wide, tall, wide, tall, wide, tall,
                        pltpu.VMEM((length, 128), jnp.float32), total, total],
        compiler_params=pltpu.CompilerParams(vmem_limit_bytes=48 * 1024 * 1024),
        cost_estimate=pl.CostEstimate(
            flops=7 * items * length * length * 256,
            bytes_accessed=4 * by_heads.size,
            transcendentals=items * length * length // 2,
        ),
    )(by_heads, grad_heads, item_base)


def sum_pair(share, axis):
    size = lax.axis_size(axis)
    if size == 2:
        other = lax.ppermute(share, axis, [(0, 1), (1, 0)])
        return share.astype(jnp.float32) + other.astype(jnp.float32)
    return lax.psum(share, axis).astype(jnp.float32)


def shards(
    block_input,
    positions,
    first_gain,
    first_shift,
    second_gain,
    second_shift,
    triple_weight,
    triple_bias,
    mixer_weight,
    output_bias,
    widen_weight,
    widen_bias,
    narrow_weight,
    cotangent,
):
    seqs, local_tokens, local_width = block_input.shape
    vectors = (first_gain, first_shift, second_gain, second_shift, output_bias, triple_bias, widen_bias)
    small = lax.all_gather(
        jnp.concatenate([vector.reshape(-1) for vector in vectors]), "fsdp", axis=0, tiled=False
    )
    groups = small.shape[0]
    pieces = []
    offset = 0
    for vector in vectors:
        pieces.append(small[:, offset : offset + vector.size].astype(jnp.float32))
        offset += vector.size
    gain_one, shift_one, gain_two, shift_two, bias_output = [
        piece.reshape(-1) for piece in pieces[:5]
    ]
    bias_triple = jnp.transpose(
        pieces[5].reshape((groups,) + triple_bias.shape), (1, 2, 0, 3)
    ).reshape(triple_bias.shape[0], triple_bias.shape[1], -1)
    bias_widen = jnp.transpose(
        pieces[6].reshape((groups,) + widen_bias.shape), (1, 0, 2)
    ).reshape(-1)
    all_positions = lax.all_gather(positions, "ctx", axis=1, tiled=True)
    whole_input = lax.all_gather(block_input, "tp", axis=2, tiled=True)
    weight_triple = lax.all_gather(triple_weight, "fsdp", axis=0, tiled=True)
    whole_cot = lax.all_gather(cotangent, "tp", axis=2, tiled=True)
    mixer_rows = mixer_weight.shape[0]
    joined = lax.all_gather(
        jnp.concatenate([mixer_weight, narrow_weight], axis=0), "fsdp", axis=1, tiled=True
    )
    weight_mixer, weight_narrow = joined[:mixer_rows], joined[mixer_rows:]
    weight_widen = lax.all_gather(widen_weight, "fsdp", axis=0, tiled=True)
    width = weight_triple.shape[0]
    heads_local, head_size = bias_triple.shape[1:]
    feature_start = lax.axis_index("tp") * local_width
    scale = head_size ** (-0.5)
    half = ROT // 2
    normed, inverse = normalize(whole_input.astype(jnp.float32))
    first_rows = (normed * gain_one + shift_one).astype(jnp.bfloat16)
    second_rows = (normed * gain_two + shift_two).astype(jnp.bfloat16)
    cosine, sine = rotary_tables(positions, ROT)
    weight_four = weight_triple.reshape(width, 3, heads_local, head_size)
    projected = jnp.einsum(
        "std,dchk->shckt", first_rows, weight_four, preferred_element_type=jnp.float32
    )
    projected = projected + jnp.transpose(bias_triple, (1, 0, 2))[None, :, :, :, None]
    turned = rotate_forward(projected[:, :, :2], cosine, sine, half)
    triple = jnp.concatenate([turned, projected[:, :, 2:]], axis=2).astype(jnp.bfloat16)
    parts = lax.axis_size("ctx")
    items = seqs * heads_local // parts
    by_heads = lax.all_to_all(
        triple.reshape(parts, items, 3, head_size, local_tokens),
        "ctx",
        split_axis=0,
        concat_axis=0,
        tiled=True,
    )
    mixer_four = weight_mixer.reshape(heads_local, head_size, width)
    mixed_grad = jnp.einsum(
        "ste,hke->shkt", whole_cot, mixer_four, preferred_element_type=jnp.float32
    ).astype(jnp.bfloat16)
    grad_heads = lax.all_to_all(
        mixed_grad.reshape(parts, items, head_size, local_tokens),
        "ctx",
        split_axis=0,
        concat_axis=0,
        tiled=True,
    )
    length = all_positions.shape[1]
    item_seq = (lax.axis_index("ctx") * items + jnp.arange(items, dtype=jnp.int32)) // heads_local
    base = (jnp.arange(length, dtype=jnp.int32)[None, :] - all_positions).astype(jnp.float32)
    item_base = jnp.take(base, item_seq, axis=0)[:, None, :]
    back_heads, mixed = attend(by_heads, grad_heads, item_base, scale)
    mixed_tokens = lax.all_to_all(
        mixed, "ctx", split_axis=0, concat_axis=0, tiled=True
    ).reshape(seqs, heads_local, head_size, local_tokens)
    back_float = (
        lax.all_to_all(back_heads, "ctx", split_axis=0, concat_axis=0, tiled=True)
        .reshape(seqs, heads_local, 3, head_size, local_tokens)
        .astype(jnp.float32)
    )
    widened = (
        jnp.einsum("std,df->stf", second_rows, weight_widen, preferred_element_type=jnp.float32)
        + bias_widen
    )
    activated_float, slope = gelu_parts(widened)
    activated = activated_float.astype(jnp.bfloat16)
    hidden_grad = (
        jnp.einsum("ste,fe->stf", whole_cot, weight_narrow, preferred_element_type=jnp.float32)
        * slope
    )
    widen_bias_grad = jnp.sum(hidden_grad, axis=(0, 1))
    hidden_rounded = hidden_grad.astype(jnp.bfloat16)
    narrow_grad = jnp.einsum(
        "stf,ste->fe", activated, whole_cot, preferred_element_type=jnp.float32
    ).astype(jnp.bfloat16)
    narrow_share = lax.psum_scatter(narrow_grad, "fsdp", scatter_dimension=1, tiled=True)
    widen_grad = jnp.einsum(
        "std,stf->df", second_rows, hidden_rounded, preferred_element_type=jnp.float32
    ).astype(jnp.bfloat16)
    widen_share = lax.psum_scatter(widen_grad, "fsdp", scatter_dimension=0, tiled=True)
    second_grad = jnp.einsum(
        "stf,df->std", hidden_rounded, weight_widen, preferred_element_type=jnp.float32
    ).astype(jnp.bfloat16)
    attention_part = jnp.einsum(
        "shkt,hke->ste", mixed_tokens, mixer_four, preferred_element_type=jnp.float32
    )
    branches = attention_part + jnp.einsum(
        "stf,fe->ste", activated, weight_narrow, preferred_element_type=jnp.float32
    )
    summed = lax.psum_scatter(
        branches.astype(jnp.bfloat16), "tp", scatter_dimension=2, tiled=True
    ).astype(jnp.float32)
    bias_slice = lax.dynamic_slice_in_dim(bias_output, feature_start, local_width, 0)
    block_output = (block_input.astype(jnp.float32) + summed + bias_slice).astype(jnp.bfloat16)
    mixer_grad = (
        jnp.einsum("shkt,ste->hke", mixed_tokens, whole_cot, preferred_element_type=jnp.float32)
        .reshape(weight_mixer.shape)
        .astype(jnp.bfloat16)
    )
    mixer_share = lax.psum_scatter(mixer_grad, "fsdp", scatter_dimension=1, tiled=True)
    unturned = rotate_back(back_float[:, :, :2], cosine, sine, half)
    projected_grad = jnp.concatenate([unturned, back_float[:, :, 2:]], axis=2)
    triple_bias_grad = jnp.transpose(jnp.sum(projected_grad, axis=(0, 4)), (1, 0, 2))
    projected_rounded = projected_grad.astype(jnp.bfloat16)
    first_grad = jnp.einsum(
        "shckt,dchk->std", projected_rounded, weight_four, preferred_element_type=jnp.float32
    ).astype(jnp.bfloat16)
    first_float = first_grad.astype(jnp.float32)
    second_float = second_grad.astype(jnp.float32)
    scaled = first_float * gain_one + second_float * gain_two
    scattered = lax.psum_scatter(
        scaled.astype(jnp.bfloat16), "tp", scatter_dimension=2, tiled=True
    ).astype(jnp.float32)
    row_sums = lax.psum(
        jnp.stack([jnp.sum(scaled, axis=-1), jnp.sum(scaled * normed, axis=-1)]), "tp"
    ) * (1.0 / width)
    triple_grad = (
        jnp.einsum(
            "std,shckt->dchk", first_rows, projected_rounded, preferred_element_type=jnp.float32
        )
        .reshape(weight_triple.shape)
        .astype(jnp.bfloat16)
    )
    triple_share = lax.psum_scatter(triple_grad, "fsdp", scatter_dimension=0, tiled=True)
    output_bias_grad = jnp.sum(whole_cot.astype(jnp.float32), axis=(0, 1))
    wide_sums = jnp.stack(
        [
            jnp.sum(first_float * normed, axis=(0, 1)),
            jnp.sum(first_float, axis=(0, 1)),
            jnp.sum(second_float * normed, axis=(0, 1)),
            jnp.sum(second_float, axis=(0, 1)),
            jnp.where(lax.axis_index("tp") == 0, output_bias_grad, 0.0),
        ]
    )
    wide_sums = lax.psum(wide_sums, ("fsdp", "ctx", "tp"))
    bias_sums = lax.psum(
        jnp.concatenate([triple_bias_grad.reshape(-1), widen_bias_grad]), ("fsdp", "ctx")
    )
    place = lax.axis_index("fsdp")
    vector_size = first_gain.shape[0]
    wide_sums = lax.dynamic_slice_in_dim(wide_sums, place * vector_size, vector_size, 1)
    triple_bias_out = lax.dynamic_slice_in_dim(
        bias_sums[: triple_bias_grad.size].reshape(triple_bias_grad.shape),
        place * triple_bias.shape[2],
        triple_bias.shape[2],
        2,
    )
    widen_bias_out = lax.dynamic_slice_in_dim(
        bias_sums[triple_bias_grad.size :].reshape(widen_bias.shape[0], -1),
        place * widen_bias.shape[1],
        widen_bias.shape[1],
        1,
    )
    own_normed = lax.dynamic_slice_in_dim(normed, feature_start, local_width, 2)
    input_grad = (
        cotangent.astype(jnp.float32)
        + inverse * (scattered - row_sums[0][..., None] - own_normed * row_sums[1][..., None])
    ).astype(jnp.bfloat16)
    return (
        block_output,
        input_grad,
        wide_sums[0],
        wide_sums[1],
        wide_sums[2],
        wide_sums[3],
        sum_pair(triple_share, "ctx"),
        triple_bias_out,
        sum_pair(mixer_share, "ctx"),
        wide_sums[4],
        sum_pair(widen_share, "ctx"),
        widen_bias_out,
        sum_pair(narrow_share, "ctx"),
    )


def solution(mesh):
    in_specs = (
        P("fsdp", "ctx", "tp"),
        P("fsdp", "ctx"),
        P("fsdp"),
        P("fsdp"),
        P("fsdp"),
        P("fsdp"),
        P("fsdp", None, "tp"),
        P(None, "tp", "fsdp"),
        P("tp", "fsdp"),
        P("fsdp"),
        P("fsdp", "tp"),
        P("tp", "fsdp"),
        P("tp", "fsdp"),
        P("fsdp", "ctx", "tp"),
    )
    out_specs = (
        P("fsdp", "ctx", "tp"),
        P("fsdp", "ctx", "tp"),
        P("fsdp"),
        P("fsdp"),
        P("fsdp"),
        P("fsdp"),
        P("fsdp", None, "tp"),
        P(None, "tp", "fsdp"),
        P("tp", "fsdp"),
        P("fsdp"),
        P("fsdp", "tp"),
        P("tp", "fsdp"),
        P("tp", "fsdp"),
    )
    return jax.shard_map(shards, mesh=mesh, in_specs=in_specs, out_specs=out_specs, check_vma=False)
```

time: 990 us -> 578 us (0.58)
  matrix products: 340 us -> 89 us
  local copies, waits for them, and re-layouts: 99 us -> 18.9 us
  waiting for transfers between devices: 256 us -> 176 us
  other arithmetic: 98.5 us -> 28.1 us
  Pallas kernels: 0 us -> 54.1 us
  blocking collectives: 159 us -> 171 us
    dot_general x28 -> x0, matrix products: 253 us -> none  [the longest x8 74.4 us: masked_scores(): jnp.einsum('idq,idk->iqk', query_block, keys_in, preferred_element_type=j...]
    psum x2 -> x0, waiting for transfers between devices: 153 us -> none  [the longest x1 153 us: shards(): lax.psum(second_grad.astype(jnp.bfloat16), 'tp').astype(jnp.float32)]
    all_gather x8 -> x0, blocking collectives: 92.5 us -> none  [the longest x1 17.8 us: shards(): lax.all_gather(mixer_weight, 'fsdp', axis=1, tiled=True)]
    psum x1 -> x3, blocking collectives: 5.27 us -> 71.4 us  [the longest x1 37.3 us: shards(): wide_sums = lax.psum(wide_sums, ('fsdp', 'ctx', 'tp'))]
    all_gather x3, waiting for transfers between devices: 0.04 us -> 60.9 us  [the longest x1 35 us: shards(): weight_triple = lax.all_gather(triple_weight, 'fsdp', axis=0, tiled=True)]
    reduce_sum x8 -> x0, other arithmetic: 58.6 us -> none  [the longest x4 33.7 us: step(): jnp.sum(jnp.exp(scores - top), axis=2, keepdims=True)]
    pallas_call x0 -> x1, Pallas kernels: none -> 54.1 us  [attend(): pl.pallas_call(functools.partial(attend_kernel, block, scale), grid=(item...]
    reduce_scatter x1, waiting for transfers between devices: 37.8 us -> 0.01 us  [shards(): lax.psum_scatter(branches.astype(jnp.bfloat16), 'tp', scatter_dimension=2...]
  transfers between devices with their start and end apart: 17 -> 18, of which waited for: 7 -> 10; matrix products, arithmetic and copies ran while one was open for 52% -> 20% of each run, Pallas kernels for 0% -> 9%
where the time goes in v1:
time: 578 us; the launch traced here: 570 us
  waiting for transfers between devices  176 us (30%)
  blocking collectives  171 us (30%)
  matrix products  89 us (15%)
  Pallas kernels  54.1 us (9%)
  other arithmetic  28.1 us (5%)
  local copies, waits for them, and re-layouts  18.9 us (3%)
  starting transfers between devices  17.1 us (3%)
  between operations  15.5 us (3%)
    pallas_call x1, Pallas kernels, attend(): pl.pallas_call(functools.partial(attend_kernel, block, scale), grid=(item...  54.1 us
    psum x1, blocking collectives, shards(): wide_sums = lax.psum(wide_sums, ('fsdp', 'ctx', 'tp'))  37.3 us
    all_to_all x1, blocking collectives, shards(): lax.all_to_all(back_heads, 'ctx', split_axis=0, concat_axis=0, tiled=True)  37 us
    all_gather x1, blocking collectives, shards(): all_positions = lax.all_gather(positions, 'ctx', axis=1, tiled=True)  35.3 us
    all_gather x1, waiting for transfers between devices, shards(): weight_triple = lax.all_gather(triple_weight, 'fsdp', axis=0, tiled=True)  35 us
    all_gather x1, waiting for transfers between devices, shards(): whole_input = lax.all_gather(block_input, 'tp', axis=2, tiled=True)  32.5 us
    unnamed x1, blocking collectives  27.7 us
    all_gather x1, waiting for transfers between devices, shards(): lax.all_gather(jnp.concatenate([mixer_weight, narrow_weight], axis=0), 'f...  25.9 us
  transfers between devices with their start and end apart: 18, of which 10 were waited for; matrix products, arithmetic and copies ran while one was open for 20% of the time, Pallas kernels for 9%

profile of v1, /device:TPU:0, one launch (start us, length us, event | category | flops | bytes accessed | tf_op | source)
XLA Modules:
  0.0 570.4 jit_solution(13089110573759211719)
XLA Ops:
  14.5 27.7 %all-reduce = bf16[6912]{0:T(1024)(128)(2,1)S(1)} all-reduce(bf16[6912]{0:T(1024)(128)(2,1)S(1)} %dynamic-update-slice), channel_id=2, replica_groups=mesh['fsdp'=4,'ctx'=2,'tp'=4] {'fsdp'}, use_global_device_ids=true, to_apply=%add | all-reduce | flops 6912 | bytes 27648
  43.4 25.9 %all-gather.11.cloned.1.call-done = bf16[1280,1024]{1,0:T(8,128)(2,1)} async-done(((bf16[1280,256]{1,0:T(8,128)(2,1)}), bf16[1280,1024]{1,0:T(8,128)(2,1)}) %all-gather.11.cloned.1.call-update) | async-done | bytes 2621456 | tf_op jit(solution)/shard_map/all_gather | solution.py:204
  70.4 32.5 %all-gather.7.cloned.1.call-done = bf16[2,1024,1024]{2,1,0:T(8,128)(2,1)} async-done(((bf16[2,1024,256]{2,1,0:T(8,128)(2,1)}), bf16[2,1024,1024]{2,1,0:T(8,128)(2,1)}) %all-gather.7.cloned.1.call-update) | async-done | bytes 4194320 | tf_op jit(solution)/shard_map/all_gather | solution.py:200
  107.8 35.0 %all-gather.9.cloned.1.call-done = bf16[1024,3,256]{0,2,1:T(8,128)(2,1)} async-done(((bf16[256,3,256]{0,2,1:T(8,128)(2,1)}), bf16[1024,3,256]{0,2,1:T(8,128)(2,1)}) %all-gather.9.cloned.1.call-update) | async-done | bytes 1572880 | tf_op jit(solution)/shard_map/all_gather | solution.py:201
  142.8 9.2 %fusion.55 = (bf16[2,4,3,64,1024]{4,3,2,1,0:T(8,128)(2,1)S(1)}, f32[2,4,3,64,1024]{4,3,2,1,0:T(8,128)}) fusion(f32[4,3,64]{2,1,0:T(4,128)S(1)} %copy.71, bf16[1024,3,4,64]{0,3,2,1:T(8,128)(2,1)} %bitcast.170, f32[1024]{0:T(1024)S(1)} %bitcast.154, f32[1024]{0:T(1024)S(1)} %bitcast.151, f32[2,1024]{1,0:T(2,128)S(1)} %add_rsqrt_fusion, ...), kind=kOutput, calls=%fused_computation.114 | convolution fusion | flops 3236954112 | bytes 15232000 | tf_op jit(solution)/shard_map/std,dchk->shckt/dot_general | solution.py:219
  153.1 24.3 %all-gather.13.cloned.1.call-done = bf16[2,1024,1024]{2,1,0:T(8,128)(2,1)} async-done(((bf16[2,1024,256]{2,1,0:T(8,128)(2,1)}), bf16[2,1024,1024]{2,1,0:T(8,128)(2,1)}) %all-gather.13.cloned.1.call-update) | async-done | bytes 4194320 | tf_op jit(solution)/shard_map/all_gather | solution.py:202
  189.8 10.0 %all-to-all-done.1.grad_ref = bf16[2,4,64,1024]{3,2,1,0:T(8,128)(2,1)S(1)} async-done(((bf16[2,4,64,1024]{3,2,1,0:T(8,128)(2,1)}), bf16[2,4,64,1024]{3,2,1,0:T(8,128)(2,1)S(1)}, u32[]{:S(2)}, u32[]{:S(2)}) %all-to-all-start.1) | async-done | bytes 1048608 | tf_op jit(solution)/shard_map/all_to_all | solution.py:238
  199.8 5.2 all-to-all-start
  205.8 35.3 %all_gather.30 = s32[2,2048]{1,0:T(2,128)S(1)} all-gather(s32[2,1024]{1,0:T(2,128)S(1)} %copy-done.18), channel_id=1, replica_groups=mesh['fsdp'=4,'ctx'=2,'tp'=4] {'ctx'}, dimensions={1}, use_global_device_ids=true | all-gather | bytes 24576 | tf_op jit(solution)/shard_map/all_gather | solution.py:199
  243.1 54.1 %shard_map.237 = (bf16[2,4,3,64,1024]{4,3,2,1,0:T(8,128)(2,1)S(1)}, bf16[2,4,64,1024]{3,2,1,0:T(8,128)(2,1)S(1)}) custom-call(bf16[2,4,3,64,1024]{4,3,2,1,0:T(8,128)(2,1)} %all-to-all-done.qkv_ref, bf16[2,4,64,1024]{3,2,1,0:T(8,128)(2,1)S(1)} %copy-done.1, f32[4,1,2048]{2,1,0:T(1,128)S(1)} %broadcast_select_fusion.base_ref), custom_call_target="tpu_custom_call" | custom-call | flops 30064771072 | bytes 6291456 | tf_op jit(solution)/shard_map/pallas_call | solution.py:128
  302.6 11.0 %multiply_convert_fusion = (bf16[2,1024,1024]{2,1,0:T(8,128)(2,1)}, f32[2,1024,1024]{2,1,0:T(8,128)}) fusion(f32[1024]{0:T(1024)S(1)} %reshape.227, bf16[1024,1024]{1,0:T(8,128)(2,1)} %all-gather.15.cloned.1.call-done, bf16[2,1024,1024]{2,1,0:T(8,128)(2,1)} %all-gather.7.cloned.1.call-done, f32[1024]{0:T(1024)S(1)} %bitcast.159, f32[1024]{0:T(1024)S(1)} %bitcast.156, ...), kind=kOutput, calls=%fused_computation.26 | convolution fusion | flops 4320133120 | bytes 18903040 | tf_op jit(solution)/shard_map/std,df->stf/dot_general | solution.py:259
  319.9 9.4 %bitcast_convert_fusion.1 = bf16[1024,1024]{1,0:T(8,128)(2,1)} fusion(bf16[2,1024,1024]{2,1,0:T(8,128)(2,1)} %get-tuple-element.96, bf16[2,1024,1024]{2,1,0:T(8,128)(2,1)} %all-gather.13.cloned.1.call-done), kind=kOutput, calls=%fused_computation.38 | convolution fusion | flops 4296015872 | bytes 10485760 | tf_op jit(solution)/shard_map/stf,ste->fe/dot_general | solution.py:270
  329.4 11.4 %fusion.56 = (f32[1024]{0:T(1024)S(1)}, bf16[2,1024,1024]{2,1,0:T(8,128)(2,1)S(1)}) fusion(f32[2,1024,1024]{2,1,0:T(8,128)} %get-tuple-element.97, f32[1024]{0:T(1024)S(1)} %reshape.227, bf16[2,1024,1024]{2,1,0:T(8,128)(2,1)} %all-gather.13.cloned.1.call-done, bf16[1280,1024]{1,0:T(8,128)(2,1)} %all-gather.11.cloned.1.call-done), kind=kOutput, calls=%fused_computation.115 | convolution fusion | flops 4320132096 | bytes 18882560 | tf_op jit(solution)/shard_map/ste,fe->stf/dot_general | solution.py:265
  342.7 7.0 %bitcast_convert_fusion.2 = bf16[1024,1024]{1,0:T(8,128)(2,1)} fusion(bf16[2,1024,1024]{2,1,0:T(8,128)(2,1)S(1)} %get-tuple-element.101, bf16[2,1024,1024]{2,1,0:T(8,128)(2,1)S(1)} %copy-done.4, f32[1024]{0:T(1024)S(1)} %bitcast.160, f32[1024]{0:T(1024)S(1)} %bitcast.157, f32[2,1024]{1,0:T(2,128)S(1)} %add_rsqrt_fusion, ...), kind=kOutput, calls=%fused_computation.39 | convolution fusion | flops 4308598784 | bytes 10510336 | tf_op jit(solution)/shard_map/std,stf->df/dot_general | solution.py:274
  349.7 37.0 %all_to_all.20 = bf16[2,4,3,64,1024]{4,3,2,1,0:T(8,128)(2,1)S(1)} all-to-all(bf16[2,4,3,64,1024]{4,3,2,1,0:T(8,128)(2,1)S(1)} %get-tuple-element.16), channel_id=1, replica_groups=mesh['fsdp'=4,'ctx'=2,'tp'=4] {'ctx'}, dimensions={0} | all-to-all | bytes 6291456 | tf_op jit(solution)/shard_map/all_to_all | solution.py:254
  395.5 7.0 %fusion.34 = f32[2,1024,1024]{2,1,0:T(8,128)S(1)} fusion(bf16[2,1024,1024]{2,1,0:T(8,128)(2,1)} %get-tuple-element.96, bf16[1280,1024]{1,0:T(8,128)(2,1)} %all-gather.11.cloned.1.call-done), kind=kOutput, calls=%fused_computation.58 | convolution fusion | flops 4294967296 | bytes 14680064 | tf_op jit(solution)/shard_map/stf,fe->ste/dot_general | solution.py:284
  407.1 6.0 %bitcast_convert_fusion = bf16[2,1024,1024]{2,1,0:T(8,128)(2,1)S(1)} fusion(bf16[1024,3,4,64,1]{0,3,2,1,4:T(8,128)(2,1)} %bitcast.171, f32[2,4,1,64,1024]{4,3,2,1,0:T(8,128)} %copy-done.7, f32[2,4,2,48,1024]{4,3,2,1,0:T(8,128)S(1)} %slice.150, f32[2,4,2,8,1024]{4,3,2,1,0:T(8,128)} %copy-done.13, f32[2,4,2,8,1024]{4,3,2,1,0:T(8,128)} %copy-done.11), kind=kOutput, calls=%fused_computation.21 | convolution fusion | flops 3235905536 | bytes 12058624 | tf_op jit(solution)/shard_map/shckt,dchk->std/dot_general | solution.py:302
  413.2 10.8 %fusion.10 = (f32[1024]{0:T(1024)S(1)}, f32[2,1024]{1,0:T(2,128)S(1)}, f32[1024]{0:T(1024)S(1)}, f32[2,1024]{1,0:T(2,128)S(1)}, f32[1024]{0:T(1024)S(1)}, /*inde...) fusion(bf16[2,1024,1024]{2,1,0:T(8,128)(2,1)S(1)} %copy-done.6, ...), kind=kOutput, calls=%fused_computation.20 | convolution fusion | flops 4334804992 | bytes 27320320 | tf_op jit(solution)/shard_map/stf,df->std/dot_general | solution.py:278
  428.4 21.4 %psum.23 = f32[1792]{0:T(1024)S(1)} all-reduce(f32[1792]{0:T(1024)S(1)} %pad_maximum_fusion.4), channel_id=1, replica_groups=mesh['fsdp'=4,'ctx'=2,'tp'=4] {'fsdp','ctx'}, use_global_device_ids=true, to_apply=%region_16.17 | all-reduce | flops 1792 | bytes 14336 | tf_op jit(solution)/shard_map/psum | solution.py:333
  450.0 37.3 %psum.22 = f32[5,1024]{1,0:T(8,128)S(1)} all-reduce(f32[5,1024]{1,0:T(8,128)S(1)} %stack.32), channel_id=1, replica_groups=mesh['fsdp'=4,'ctx'=2,'tp'=4] {'fsdp','ctx','tp'}, use_global_device_ids=true, to_apply=%region_12.13 | all-reduce | flops 5120 | bytes 40960 | tf_op jit(solution)/shard_map/psum | solution.py:332
  487.3 12.8 %psum.21 = f32[2,2,1024]{2,1,0:T(2,128)S(1)} all-reduce(f32[2,2,1024]{2,1,0:T(2,128)S(1)} %pad_maximum_fusion.3), channel_id=1, replica_groups=mesh['fsdp'=4,'ctx'=2,'tp'=4] {'tp'}, use_global_device_ids=true, to_apply=%region_6.7 | all-reduce | flops 4096 | bytes 32768 | tf_op jit(solution)/shard_map/psum | solution.py:311
  507.2 8.1 %collective-permute-done.3 = bf16[1024,256]{1,0:T(8,128)(2,1)S(1)} collective-permute-done((bf16[1024,256]{1,0:T(8,128)(2,1)}, bf16[1024,256]{1,0:T(8,128)(2,1)S(1)}, u32[]{:S(2)}, u32[]{:S(2)}) %collective-permute-start.3) | collective-permute-done | bytes 524320 | tf_op jit(solution)/shard_map/ppermute | solution.py:158
  517.4 9.1 %collective-permute-done.2 = bf16[256,1024]{1,0:T(8,128)(2,1)S(1)} collective-permute-done((bf16[256,1024]{1,0:T(8,128)(2,1)}, bf16[256,1024]{1,0:T(8,128)(2,1)S(1)}, u32[]{:S(2)}, u32[]{:S(2)}) %collective-permute-start.2) | collective-permute-done | bytes 524320 | tf_op jit(solution)/shard_map/ppermute | solution.py:158
  537.0 23.6 %reduce-scatter.9.cloned.1.call-done = bf16[2,1024,256]{2,1,0:T(8,128)(2,1)} async-done(((bf16[2,1024,1024]{2,1,0:T(8,128)(2,1)}), bf16[2,1024,256]{2,1,0:T(8,128)(2,1)}) %reduce-scatter.9.cloned.1.call-update) | async-done | bytes 1048592 | tf_op jit(solution)/shard_map/reduce_scatter | solution.py:308
  (174 shorter events, 83.9 us)
Async XLA Ops:
  7.3 62.0 %all-gather.11.cloned.1.call-start = ((), (), s32[]{:S(2)}) async-start(), calls=%async_computation.12 | async-start | bytes 3276800 | tf_op jit(solution)/shard_map/all_gather | solution.py:204
  9.3 93.6 %all-gather.7.cloned.1.call-start = ((), (), s32[]{:S(2)}) async-start(), calls=%async_computation.10 | async-start | bytes 5242880 | tf_op jit(solution)/shard_map/all_gather | solution.py:200
  10.1 132.7 %all-gather.9.cloned.1.call-start = ((), (), s32[]{:S(2)}) async-start(), calls=%async_computation.11 | async-start | bytes 1966080 | tf_op jit(solution)/shard_map/all_gather | solution.py:201
  12.1 165.4 %all-gather.13.cloned.1.call-start = ((), (), s32[]{:S(2)}) async-start(), calls=%async_computation.13 | async-start | bytes 5242880 | tf_op jit(solution)/shard_map/all_gather | solution.py:202
  70.4 107.1 %copy-start.15 = (bf16[256,1024]{1,0:T(8,128)(2,1)}, bf16[256,1024]{1,0:T(8,128)(2,1)S(1)}, u32[]{:S(2)}) copy-start(bf16[256,1024]{1,0:T(8,128)(2,1)S(1)} %slice.142) | copy-start | bytes 1572868
  181.9 17.9 %all-to-all-start.1 = ((bf16[2,4,64,1024]{3,2,1,0:T(8,128)(2,1)}), bf16[2,4,64,1024]{3,2,1,0:T(8,128)(2,1)S(1)}, u32[]{:S(2)}, u32[]{:S(2)}) async-start(bf16[2,4,64,1024]{3,2,1,0:T(8,128)(2,1)} %fusion.42), calls=%async_computation.1 | async-start | bytes 2097152 | tf_op jit(solution)/shard_map/all_to_all | solution.py:238
  199.8 42.1 %copy-start = (bf16[2,4,64,1024]{3,2,1,0:T(8,128)(2,1)}, bf16[2,4,64,1024]{3,2,1,0:T(8,128)(2,1)S(1)}, u32[]{:S(2)}) copy-start(bf16[2,4,64,1024]{3,2,1,0:T(8,128)(2,1)S(1)} %all-to-all-done.1.grad_ref) | copy-start | bytes 3145732
  199.8 42.1 %all-to-all-start = ((bf16[2,4,3,64,1024]{4,3,2,1,0:T(8,128)(2,1)}), bf16[2,4,3,64,1024]{4,3,2,1,0:T(8,128)(2,1)}, u32[]{:S(2)}, u32[]{:S(2)}) async-start(bf16[2,4,3,64,1024]{4,3,2,1,0:T(8,128)(2,1)} %pad_maximum_fusion.1), calls=%async_computation | async-start | bytes 6291456 | tf_op jit(solution)/shard_map/all_to_all | solution.py:227
  205.0 97.6 %all-gather.15.cloned.1.call-start = ((), (), s32[]{:S(2)}) async-start(), calls=%async_computation.14 | async-start | bytes 2621440 | tf_op jit(solution)/shard_map/all_gather | solution.py:208
  298.1 17.2 %all-to-all-start.2 = ((bf16[2,4,64,1024]{3,2,1,0:T(8,128)(2,1)}), bf16[2,4,64,1024]{3,2,1,0:T(8,128)(2,1)}, u32[]{:S(2)}, u32[]{:S(2)}) async-start(bf16[2,4,64,1024]{3,2,1,0:T(8,128)(2,1)} %copy-done.2), calls=%async_computation.2 | async-start | bytes 2097152 | tf_op jit(solution)/shard_map/all_to_all | solution.py:250
  302.5 147.4 %reduce-scatter.13.cloned.1.call-start = ((), (), s32[]{:S(2)}) async-start(), calls=%async_computation.18 | async-start | bytes 655360 | tf_op jit(solution)/shard_map/reduce_scatter | solution.py:297
  319.8 180.3 %reduce-scatter.17.cloned.1.call-start = ((), (), s32[]{:S(2)}) async-start(), calls=%async_computation.20 | async-start | bytes 2621440 | tf_op jit(solution)/shard_map/reduce_scatter | solution.py:273
  329.3 173.5 %reduce-scatter.15.cloned.1.call-start = ((), (), s32[]{:S(2)}) async-start(), calls=%async_computation.19 | async-start | bytes 2621440 | tf_op jit(solution)/shard_map/reduce_scatter | solution.py:277
  329.3 13.4 %copy-start.4 = (bf16[2,1024,1024]{2,1,0:T(8,128)(2,1)S(1)}, bf16[2,1024,1024]{2,1,0:T(8,128)(2,1)}, u32[]{:S(2)}) copy-start(bf16[2,1024,1024]{2,1,0:T(8,128)(2,1)} %all-gather.7.cloned.1.call-done) | copy-start | bytes 12582916
  349.7 156.2 %reduce-scatter.11.cloned.1.call-start = ((), (), s32[]{:S(2)}) async-start(), calls=%async_computation.17 | async-start | bytes 1966080 | tf_op jit(solution)/shard_map/reduce_scatter | solution.py:321
  395.4 138.8 %reduce-scatter.7.cloned.1.call-start = ((), (), s32[]{:S(2)}) async-start(), calls=%async_computation.15 | async-start | bytes 5242880 | tf_op jit(solution)/shard_map/reduce_scatter | solution.py:287
  407.0 153.5 %reduce-scatter.9.cloned.1.call-start = ((), (), s32[]{:S(2)}) async-start(), calls=%async_computation.16 | async-start | bytes 5242880 | tf_op jit(solution)/shard_map/reduce_scatter | solution.py:308
  428.3 105.9 %copy-start.9 = (bf16[2,1024,256]{2,1,0:T(8,128)(2,1)S(1)}, bf16[2,1024,256]{2,1,0:T(8,128)(2,1)}, u32[]{:S(2)}) copy-start(bf16[2,1024,256]{2,1,0:T(8,128)(2,1)} %param.14) | copy-start | bytes 3145732
  450.0 54.3 %collective-permute-start.1 = (bf16[256,256]{1,0:T(8,128)(2,1)}, bf16[256,256]{1,0:T(8,128)(2,1)S(1)}, u32[]{:S(2)}, u32[]{:S(2)}) collective-permute-start(bf16[256,256]{1,0:T(8,128)(2,1)} %reduce-scatter.13.cloned.1.call-done), channel_id=1, source_target_pairs={{0,4},{4,0},{1,5},{5,1},{2,6},{6,2},{3,7},{7,3},{8,12},{12,8},{9,1... | collective-permute-start | bytes 393224 | tf_op jit(solution)/shard_map/ppermute | solution.py:158
  500.2 15.1 %collective-permute-start.3 = (bf16[1024,256]{1,0:T(8,128)(2,1)}, bf16[1024,256]{1,0:T(8,128)(2,1)S(1)}, u32[]{:S(2)}, u32[]{:S(2)}) collective-permute-start(bf16[1024,256]{1,0:T(8,128)(2,1)} %reduce-scatter.17.cloned.1.call-done), channel_id=1, source_target_pairs={{0,4},{4,0},{1,5},{5,1},{2,6},{6,2},{3,7},{7,3},{8,12},{12,8},{9,1... | collective-permute-start | bytes 1572872 | tf_op jit(solution)/shard_map/ppermute | solution.py:158
  502.8 23.7 %collective-permute-start.2 = (bf16[256,1024]{1,0:T(8,128)(2,1)}, bf16[256,1024]{1,0:T(8,128)(2,1)S(1)}, u32[]{:S(2)}, u32[]{:S(2)}) collective-permute-start(bf16[256,1024]{1,0:T(8,128)(2,1)} %reduce-scatter.15.cloned.1.call-done), channel_id=1, source_target_pairs={{0,4},{4,0},{1,5},{5,1},{2,6},{6,2},{3,7},{7,3},{8,12},{12,8},{9,1... | collective-permute-start | bytes 1572872 | tf_op jit(solution)/shard_map/ppermute | solution.py:158
  505.9 27.1 %copy-start.17 = (bf16[256,3,256]{0,2,1:T(8,128)(2,1)S(1)}, bf16[256,3,256]{0,2,1:T(8,128)(2,1)}, u32[]{:S(2)}) copy-start(bf16[256,3,256]{0,2,1:T(8,128)(2,1)} %reduce-scatter.11.cloned.1.call-done) | copy-start | bytes 1179652
  505.9 27.1 %collective-permute-start = (bf16[256,3,256]{0,2,1:T(8,128)(2,1)}, bf16[256,3,256]{0,2,1:T(8,128)(2,1)S(1)}, u32[]{:S(2)}, u32[]{:S(2)}) collective-permute-start(bf16[256,3,256]{0,2,1:T(8,128)(2,1)} %reduce-scatter.11.cloned.1.call-done), channel_id=1, source_target_pairs={{0,4},{4,0},{1,5},{5,1},{2,6},{6,2},{3,7},{7,3},{8,12},{12,8},{9,1... | collective-permute-start | bytes 1179656 | tf_op jit(solution)/shard_map/ppermute | solution.py:158
  517.4 43.1 %copy-start.10 = (bf16[2,1024,256]{2,1,0:T(8,128)(2,1)S(1)}, bf16[2,1024,256]{2,1,0:T(8,128)(2,1)}, u32[]{:S(2)}) copy-start(bf16[2,1024,256]{2,1,0:T(8,128)(2,1)} %param.27) | copy-start | bytes 3145732
  (25 other events, 115.4 us)
Sparse Core Ops, SparseCore 0:
  10.2 59.0 all-gather.10
  70.8 32.0 all-gather.6
  105.1 37.6 all-gather.8
  144.2 33.2 all-gather.12
  207.1 46.1 all-gather.14
  320.0 20.9 reduce-scatter.12
  343.2 41.8 reduce-scatter.16
  387.5 42.8 reduce-scatter.14
  432.6 34.6 reduce-scatter.10
  469.7 43.7 reduce-scatter.6
  516.1 44.3 reduce-scatter.8
